TPU v7x, 256 devices: a whole 4x4x8 slice. The times are simulated.
256 devices in a mesh: group: 16 (over x_lo, y, core), dp: 16 (over x_hi, z).
Axes of the slice: x: 4 (x_hi: 2, x_lo: 2; x = x_hi * 2 + x_lo), y: 4, z: 8, core: 2. Of those that a mesh axis runs over, the one named last changes fastest.
Arguments:
- latents: bfloat16 [16, 512, 6144], P('group', 'dp'), may hold values from -6 to 6
- steps: int32 [16], P('group'), may hold values from 0 to 15
- segment_ids: int32 [512], replicated, may hold values from 0 to 15, never falling along the last dimension, each value on 1 to 64 neighbouring positions
- mod_table: float32 [16, 2, 6144], replicated, may hold values from -3 to 3
- w_query: bfloat16 [6144, 4096], P(None, 'dp')
- w_key: bfloat16 [6144, 4096], P(None, 'dp')
- w_value: bfloat16 [6144, 4096], P(None, 'dp'), may hold values from -0.3125 to 0.3125
Outputs:
- attended: bfloat16 [16, 512, 4096], P('group', 'dp')
Inputs may be any that keep to these rules, and one draw needn't show every extreme that they name: `segment_ids`: rows of one clip are contiguous; every clip index occurs, a clip holds 1 to 64 rows and one holds exactly that many.
All inputs are finite; a program needn't handle non-finite values.
Results may differ from a plain program's by a relative error of at most 0.011.
Values may be sent and summed in bfloat16 or wider, within the bound.
A program may use at most 128 MiB of HBM per device.

v0:
```python
import math
import jax
import jax.numpy as jnp
from jax import lax
from jax.sharding import PartitionSpec as P

D = 6144
HD = 128
HEAD_DEV = 2
STEPS = 16


def in_one_piece(arrays, axis, dim, along):
    both = jnp.concatenate(arrays, axis=along)
    out, at, gathered = (lax.all_gather(both, axis, axis=dim, tiled=True), 0, [])
    for a in arrays:
        gathered.append(lax.slice_in_dim(out, at, at + a.shape[along], axis=along))
        at += a.shape[along]
    return tuple(gathered)


def per_device(latents, steps, segment_ids, mod_table, w_query, w_key, w_value):
    rows_here = latents.shape[1]
    tokc = rows_here * lax.axis_size("dp")
    width = HEAD_DEV * HD
    x = latents[0].astype(jnp.float32)
    normed = x * lax.rsqrt(jnp.mean(x * x, axis=-1, keepdims=True) + 1e-06)
    picker = (steps[:, None] == jnp.arange(STEPS, dtype=jnp.int32)[None, :]).astype(jnp.float32)
    modulation = jnp.dot(picker, mod_table.reshape(STEPS, 2 * D), precision=lax.Precision.HIGHEST)
    modulated = (normed * (1.0 + modulation[:, :D]) + modulation[:, D:]).astype(jnp.bfloat16)
    piece = lax.all_gather(modulated, "dp", axis=0, tiled=True)
    first = jnp.dot(piece, w_query, preferred_element_type=jnp.float32).astype(jnp.bfloat16)
    second = jnp.dot(piece, w_key, preferred_element_type=jnp.float32).astype(jnp.bfloat16)
    third = jnp.dot(piece, w_value, preferred_element_type=jnp.float32).astype(jnp.bfloat16)
    projected = jnp.concatenate([first, second, third], axis=1)
    query = projected[:, :width].reshape(tokc, HEAD_DEV, HD)
    keys_own = projected[:, width : 2 * width]
    values_own = projected[:, 2 * width :]
    mine = lax.axis_index("group")
    same_clip = segment_ids[:, None] == segment_ids[None, :]
    inverse = 1.0 / math.sqrt(HD)

    def update(carry, key_block, value_block):
        best, total, accum = carry
        scores = (
            jnp.einsum(
                "thd,khd->htk",
                query,
                key_block.reshape(tokc, HEAD_DEV, HD),
                preferred_element_type=jnp.float32,
            )
            * inverse
        )
        scores = jnp.where(same_clip[None], scores, -1e30)
        new_best = jnp.maximum(best, jnp.max(scores, axis=-1))
        weights = jnp.where(same_clip[None], jnp.exp(scores - new_best[:, :, None]), 0.0)
        fade = jnp.exp(best - new_best)
        total = total * fade + jnp.sum(weights, axis=-1)
        added = jnp.einsum(
            "htk,khd->thd",
            weights.astype(jnp.bfloat16),
            value_block.reshape(tokc, HEAD_DEV, HD),
            preferred_element_type=jnp.float32,
        )
        accum = accum * jnp.transpose(fade)[:, :, None] + added
        return (new_best, total, accum)

    def visit(carry, key_block, value_block, source):
        usable = jnp.logical_and(source <= mine, source >= 0)
        return lax.cond(
            usable, lambda state: update(state, key_block, value_block), lambda state: state, carry
        )

    start_state = (
        jnp.full((HEAD_DEV, tokc), -1e30, jnp.float32),
        jnp.zeros((HEAD_DEV, tokc), jnp.float32),
        jnp.zeros((tokc, HEAD_DEV, HD), jnp.float32),
    )
    piece = in_one_piece((keys_own, values_own), "group", 0, 1)
    count = piece[0].shape[0] // tokc

    def single(index, state):
        key_block = lax.dynamic_slice_in_dim(piece[0], index * tokc, tokc, 0)
        value_block = lax.dynamic_slice_in_dim(piece[1], index * tokc, tokc, 0)
        return visit(state, key_block, value_block, index)

    carry = lax.fori_loop(0, count, single, start_state)
    best, total, accum = carry
    result = (accum / jnp.transpose(total)[:, :, None]).reshape(tokc, width).astype(jnp.bfloat16)
    regrouped = lax.all_to_all(result, "dp", split_axis=0, concat_axis=1, tiled=True)
    return regrouped[None]


def solution(mesh):
    placed = (
        P("group", "dp", None),
        P("group"),
        P(),
        P(),
        P(None, "dp"),
        P(None, "dp"),
        P(None, "dp"),
    )
    return jax.shard_map(
        per_device, mesh=mesh, in_specs=placed, out_specs=P("group", "dp", None), check_vma=False
    )
```

profile of v0, /device:TPU:27, one launch (start us, length us, event | category | flops | bytes accessed | tf_op | source)
XLA Modules:
  0.0 297.3 jit_solution(8042137725669814860)
XLA Ops:
  11.7 116.8 %all-gather.3.cloned.1.call-done = bf16[512,6144]{1,0:T(8,128)(2,1)} async-done(((bf16[32,6144]{1,0:T(8,128)(2,1)}), bf16[512,6144]{1,0:T(8,128)(2,1)}) %all-gather.3.cloned.1.call-update) | async-done | bytes 6291472 | tf_op jit(solution)/shard_map/all_gather | solution.py:31
  128.5 4.8 %convolution_convert_fusion.1 = bf16[512,256]{0,1:T(8,128)(2,1)S(1)} fusion(bf16[512,6144]{1,0:T(8,128)(2,1)} %all-gather.3.cloned.1.call-done, bf16[6144,256]{1,0:T(8,128)(2,1)S(1)} %copy-done), kind=kOutput, calls=%fused_computation.22 | convolution fusion | flops 1610743808 | bytes 9699328 | tf_op jit(solution)/shard_map/dot_general | solution.py:34
  134.0 1.8 convolution_convert_fusion.2
  136.7 6.3 %convolution_convert_fusion = bf16[512,256]{0,1:T(8,128)(2,1)} fusion(bf16[512,6144]{1,0:T(8,128)(2,1)} %all-gather.3.cloned.1.call-done, bf16[6144,256]{1,0:T(8,128)(2,1)} %param.15), kind=kOutput, calls=%fused_computation.21 | convolution fusion | flops 1610743808 | bytes 9699328 | tf_op jit(solution)/shard_map/dot_general | solution.py:32
  144.1 45.9 %all-gather.5.cloned.1.call-done = bf16[8192,512]{0,1:T(8,128)(2,1)} async-done(((bf16[512,512]{0,1:T(8,128)(2,1)}), bf16[8192,512]{0,1:T(8,128)(2,1)}) %all-gather.5.cloned.1.call-update) | async-done | bytes 8388624 | tf_op jit(solution)/shard_map/all_gather | solution.py:15
  190.0 5.9 %fusion.24 = (bf16[8192,256]{0,1:T(8,128)(2,1)}, bf16[8192,256]{0,1:T(8,128)(2,1)}) fusion(bf16[8192,512]{0,1:T(8,128)(2,1)} %all-gather.5.cloned.1.call-done), kind=kLoop, calls=%fused_computation.39 | loop fusion | bytes 16777216 | tf_op jit(solution)/shard_map/slice | solution.py:17
  196.7 72.6 %while.18 = (s32[]{:T(128)}, f32[2,512]{1,0:T(2,128)S(1)}, f32[2,512]{1,0:T(2,128)S(1)}, f32[512,2,128]{2,0,1:T(8,128)}, s32[]{:T(128)}, /*index=5*/bf16[8192,25...) while((s32[]{:T(128)}, f32[2,512]{1,0:T(2,128)S(1)}, ...), condition=%wide.region_6.7_spmd.clone, body=%wide.region_1.6_spmd.clone.sunk | while | flops 275778560 | bytes 14487929 | solution.py:87
  196.7 4.5 %conditional.3 = ((f32[2,512]{1,0:T(2,128)S(1)}, f32[2,512]{1,0:T(2,128)S(1)}, f32[512,2,128]{2,0,1:T(8,128)})) conditional(s32[]{:T(128)} %convert_element_type.58, (f32[2,512]{1,0:T(2,128)S(1)}, f32[2,512]{1,0:T(2,128)S(1)}, f32[512,2,128]{2,0,1:T(8,128)}) %tuple.61, (s32[512]{0:T(512)S(1)}, s32[]{:T(128)}, bf16[8192,256]{0,1:T(8,128)(2,1)}, ...), branch_computations={%region_2.0_spmd, %region_3.5_spmd} | conditional | flops 275778560 | bytes 14487690 | solution.py:70
  201.2 4.5 %conditional.3 = ((f32[2,512]{1,0:T(2,128)S(1)}, f32[2,512]{1,0:T(2,128)S(1)}, f32[512,2,128]{2,0,1:T(8,128)})) conditional(s32[]{:T(128)} %convert_element_type.58, (f32[2,512]{1,0:T(2,128)S(1)}, f32[2,512]{1,0:T(2,128)S(1)}, f32[512,2,128]{2,0,1:T(8,128)}) %tuple.61, (s32[512]{0:T(512)S(1)}, s32[]{:T(128)}, bf16[8192,256]{0,1:T(8,128)(2,1)}, ...), branch_computations={%region_2.0_spmd, %region_3.5_spmd} | conditional | flops 275778560 | bytes 14487690 | solution.py:70
  205.7 4.5 %conditional.3 = ((f32[2,512]{1,0:T(2,128)S(1)}, f32[2,512]{1,0:T(2,128)S(1)}, f32[512,2,128]{2,0,1:T(8,128)})) conditional(s32[]{:T(128)} %convert_element_type.58, (f32[2,512]{1,0:T(2,128)S(1)}, f32[2,512]{1,0:T(2,128)S(1)}, f32[512,2,128]{2,0,1:T(8,128)}) %tuple.61, (s32[512]{0:T(512)S(1)}, s32[]{:T(128)}, bf16[8192,256]{0,1:T(8,128)(2,1)}, ...), branch_computations={%region_2.0_spmd, %region_3.5_spmd} | conditional | flops 275778560 | bytes 14487690 | solution.py:70
  210.3 4.5 %conditional.3 = ((f32[2,512]{1,0:T(2,128)S(1)}, f32[2,512]{1,0:T(2,128)S(1)}, f32[512,2,128]{2,0,1:T(8,128)})) conditional(s32[]{:T(128)} %convert_element_type.58, (f32[2,512]{1,0:T(2,128)S(1)}, f32[2,512]{1,0:T(2,128)S(1)}, f32[512,2,128]{2,0,1:T(8,128)}) %tuple.61, (s32[512]{0:T(512)S(1)}, s32[]{:T(128)}, bf16[8192,256]{0,1:T(8,128)(2,1)}, ...), branch_computations={%region_2.0_spmd, %region_3.5_spmd} | conditional | flops 275778560 | bytes 14487690 | solution.py:70
  214.8 4.5 %conditional.3 = ((f32[2,512]{1,0:T(2,128)S(1)}, f32[2,512]{1,0:T(2,128)S(1)}, f32[512,2,128]{2,0,1:T(8,128)})) conditional(s32[]{:T(128)} %convert_element_type.58, (f32[2,512]{1,0:T(2,128)S(1)}, f32[2,512]{1,0:T(2,128)S(1)}, f32[512,2,128]{2,0,1:T(8,128)}) %tuple.61, (s32[512]{0:T(512)S(1)}, s32[]{:T(128)}, bf16[8192,256]{0,1:T(8,128)(2,1)}, ...), branch_computations={%region_2.0_spmd, %region_3.5_spmd} | conditional | flops 275778560 | bytes 14487690 | solution.py:70
  219.4 4.5 %conditional.3 = ((f32[2,512]{1,0:T(2,128)S(1)}, f32[2,512]{1,0:T(2,128)S(1)}, f32[512,2,128]{2,0,1:T(8,128)})) conditional(s32[]{:T(128)} %convert_element_type.58, (f32[2,512]{1,0:T(2,128)S(1)}, f32[2,512]{1,0:T(2,128)S(1)}, f32[512,2,128]{2,0,1:T(8,128)}) %tuple.61, (s32[512]{0:T(512)S(1)}, s32[]{:T(128)}, bf16[8192,256]{0,1:T(8,128)(2,1)}, ...), branch_computations={%region_2.0_spmd, %region_3.5_spmd} | conditional | flops 275778560 | bytes 14487690 | solution.py:70
  223.9 4.5 %conditional.3 = ((f32[2,512]{1,0:T(2,128)S(1)}, f32[2,512]{1,0:T(2,128)S(1)}, f32[512,2,128]{2,0,1:T(8,128)})) conditional(s32[]{:T(128)} %convert_element_type.58, (f32[2,512]{1,0:T(2,128)S(1)}, f32[2,512]{1,0:T(2,128)S(1)}, f32[512,2,128]{2,0,1:T(8,128)}) %tuple.61, (s32[512]{0:T(512)S(1)}, s32[]{:T(128)}, bf16[8192,256]{0,1:T(8,128)(2,1)}, ...), branch_computations={%region_2.0_spmd, %region_3.5_spmd} | conditional | flops 275778560 | bytes 14487690 | solution.py:70
  228.4 4.5 %conditional.3 = ((f32[2,512]{1,0:T(2,128)S(1)}, f32[2,512]{1,0:T(2,128)S(1)}, f32[512,2,128]{2,0,1:T(8,128)})) conditional(s32[]{:T(128)} %convert_element_type.58, (f32[2,512]{1,0:T(2,128)S(1)}, f32[2,512]{1,0:T(2,128)S(1)}, f32[512,2,128]{2,0,1:T(8,128)}) %tuple.61, (s32[512]{0:T(512)S(1)}, s32[]{:T(128)}, bf16[8192,256]{0,1:T(8,128)(2,1)}, ...), branch_computations={%region_2.0_spmd, %region_3.5_spmd} | conditional | flops 275778560 | bytes 14487690 | solution.py:70
  233.0 4.5 %conditional.3 = ((f32[2,512]{1,0:T(2,128)S(1)}, f32[2,512]{1,0:T(2,128)S(1)}, f32[512,2,128]{2,0,1:T(8,128)})) conditional(s32[]{:T(128)} %convert_element_type.58, (f32[2,512]{1,0:T(2,128)S(1)}, f32[2,512]{1,0:T(2,128)S(1)}, f32[512,2,128]{2,0,1:T(8,128)}) %tuple.61, (s32[512]{0:T(512)S(1)}, s32[]{:T(128)}, bf16[8192,256]{0,1:T(8,128)(2,1)}, ...), branch_computations={%region_2.0_spmd, %region_3.5_spmd} | conditional | flops 275778560 | bytes 14487690 | solution.py:70
  237.5 4.5 %conditional.3 = ((f32[2,512]{1,0:T(2,128)S(1)}, f32[2,512]{1,0:T(2,128)S(1)}, f32[512,2,128]{2,0,1:T(8,128)})) conditional(s32[]{:T(128)} %convert_element_type.58, (f32[2,512]{1,0:T(2,128)S(1)}, f32[2,512]{1,0:T(2,128)S(1)}, f32[512,2,128]{2,0,1:T(8,128)}) %tuple.61, (s32[512]{0:T(512)S(1)}, s32[]{:T(128)}, bf16[8192,256]{0,1:T(8,128)(2,1)}, ...), branch_computations={%region_2.0_spmd, %region_3.5_spmd} | conditional | flops 275778560 | bytes 14487690 | solution.py:70
  242.1 4.5 %conditional.3 = ((f32[2,512]{1,0:T(2,128)S(1)}, f32[2,512]{1,0:T(2,128)S(1)}, f32[512,2,128]{2,0,1:T(8,128)})) conditional(s32[]{:T(128)} %convert_element_type.58, (f32[2,512]{1,0:T(2,128)S(1)}, f32[2,512]{1,0:T(2,128)S(1)}, f32[512,2,128]{2,0,1:T(8,128)}) %tuple.61, (s32[512]{0:T(512)S(1)}, s32[]{:T(128)}, bf16[8192,256]{0,1:T(8,128)(2,1)}, ...), branch_computations={%region_2.0_spmd, %region_3.5_spmd} | conditional | flops 275778560 | bytes 14487690 | solution.py:70
  246.6 4.5 %conditional.3 = ((f32[2,512]{1,0:T(2,128)S(1)}, f32[2,512]{1,0:T(2,128)S(1)}, f32[512,2,128]{2,0,1:T(8,128)})) conditional(s32[]{:T(128)} %convert_element_type.58, (f32[2,512]{1,0:T(2,128)S(1)}, f32[2,512]{1,0:T(2,128)S(1)}, f32[512,2,128]{2,0,1:T(8,128)}) %tuple.61, (s32[512]{0:T(512)S(1)}, s32[]{:T(128)}, bf16[8192,256]{0,1:T(8,128)(2,1)}, ...), branch_computations={%region_2.0_spmd, %region_3.5_spmd} | conditional | flops 275778560 | bytes 14487690 | solution.py:70
  251.1 4.5 %conditional.3 = ((f32[2,512]{1,0:T(2,128)S(1)}, f32[2,512]{1,0:T(2,128)S(1)}, f32[512,2,128]{2,0,1:T(8,128)})) conditional(s32[]{:T(128)} %convert_element_type.58, (f32[2,512]{1,0:T(2,128)S(1)}, f32[2,512]{1,0:T(2,128)S(1)}, f32[512,2,128]{2,0,1:T(8,128)}) %tuple.61, (s32[512]{0:T(512)S(1)}, s32[]{:T(128)}, bf16[8192,256]{0,1:T(8,128)(2,1)}, ...), branch_computations={%region_2.0_spmd, %region_3.5_spmd} | conditional | flops 275778560 | bytes 14487690 | solution.py:70
  255.7 4.5 %conditional.3 = ((f32[2,512]{1,0:T(2,128)S(1)}, f32[2,512]{1,0:T(2,128)S(1)}, f32[512,2,128]{2,0,1:T(8,128)})) conditional(s32[]{:T(128)} %convert_element_type.58, (f32[2,512]{1,0:T(2,128)S(1)}, f32[2,512]{1,0:T(2,128)S(1)}, f32[512,2,128]{2,0,1:T(8,128)}) %tuple.61, (s32[512]{0:T(512)S(1)}, s32[]{:T(128)}, bf16[8192,256]{0,1:T(8,128)(2,1)}, ...), branch_computations={%region_2.0_spmd, %region_3.5_spmd} | conditional | flops 275778560 | bytes 14487690 | solution.py:70
  260.2 4.5 %conditional.3 = ((f32[2,512]{1,0:T(2,128)S(1)}, f32[2,512]{1,0:T(2,128)S(1)}, f32[512,2,128]{2,0,1:T(8,128)})) conditional(s32[]{:T(128)} %convert_element_type.58, (f32[2,512]{1,0:T(2,128)S(1)}, f32[2,512]{1,0:T(2,128)S(1)}, f32[512,2,128]{2,0,1:T(8,128)}) %tuple.61, (s32[512]{0:T(512)S(1)}, s32[]{:T(128)}, bf16[8192,256]{0,1:T(8,128)(2,1)}, ...), branch_computations={%region_2.0_spmd, %region_3.5_spmd} | conditional | flops 275778560 | bytes 14487690 | solution.py:70
  264.7 4.5 %conditional.3 = ((f32[2,512]{1,0:T(2,128)S(1)}, f32[2,512]{1,0:T(2,128)S(1)}, f32[512,2,128]{2,0,1:T(8,128)})) conditional(s32[]{:T(128)} %convert_element_type.58, (f32[2,512]{1,0:T(2,128)S(1)}, f32[2,512]{1,0:T(2,128)S(1)}, f32[512,2,128]{2,0,1:T(8,128)}) %tuple.61, (s32[512]{0:T(512)S(1)}, s32[]{:T(128)}, bf16[8192,256]{0,1:T(8,128)(2,1)}, ...), branch_computations={%region_2.0_spmd, %region_3.5_spmd} | conditional | flops 275778560 | bytes 14487690 | solution.py:70
  271.7 17.8 %all_to_all.13 = bf16[16,32,256]{2,1,0:T(8,128)(2,1)S(1)} all-to-all(bf16[16,32,256]{2,1,0:T(8,128)(2,1)} %convert_element_type.47), channel_id=1, replica_groups=mesh['group'=16,'dp'=16] {'dp'}, dimensions={0} | all-to-all | bytes 524288 | tf_op jit(solution)/shard_map/all_to_all | solution.py:90
  (222 shorter events, 82.0 us)
Async XLA Ops:
  6.5 121.9 %copy-start = (bf16[6144,256]{1,0:T(8,128)(2,1)S(1)}, bf16[6144,256]{1,0:T(8,128)(2,1)}, u32[]{:S(2)}) copy-start(bf16[6144,256]{1,0:T(8,128)(2,1)} %param.17) | copy-start | bytes 9437188
  6.5 4.1 %copy-start.3 = (bf16[1,32,6144]{2,1,0:T(8,128)(2,1)S(1)}, bf16[1,32,6144]{2,1,0:T(8,128)(2,1)}, u32[]{:S(2)}) copy-start(bf16[1,32,6144]{2,1,0:T(8,128)(2,1)} %param.11) | copy-start | bytes 1179652
  6.5 121.9 %all-gather.3.cloned.1.call-start = ((), (), s32[]{:S(2)}) async-start(), calls=%async_computation.1 | async-start | bytes 6684672 | tf_op jit(solution)/shard_map/all_gather | solution.py:31
  11.6 178.3 %all-gather.5.cloned.1.call-start = ((), (), s32[]{:S(2)}) async-start(), calls=%async_computation.2 | async-start | bytes 8912896 | tf_op jit(solution)/shard_map/all_gather | solution.py:15
  128.4 4.8 %copy-start.5 = (bf16[512,6144]{1,0:T(8,128)(2,1)S(1)}, bf16[512,6144]{1,0:T(8,128)(2,1)}, u32[]{:S(2)}) copy-start(bf16[512,6144]{1,0:T(8,128)(2,1)} %all-gather.3.cloned.1.call-done) | copy-start | bytes 18874372
  128.4 5.5 %copy-start.6 = (bf16[6144,256]{1,0:T(8,128)(2,1)S(1)}, bf16[6144,256]{1,0:T(8,128)(2,1)}, u32[]{:S(2)}) copy-start(bf16[6144,256]{1,0:T(8,128)(2,1)} %param.16) | copy-start | bytes 9437188
  144.0 52.6 %copy-start.4 = (s32[512]{0:T(512)S(1)}, s32[512]{0:T(512)}, u32[]{:S(2)}) copy-start(s32[512]{0:T(512)} %param.13) | copy-start | bytes 6148
  196.9 2.4 copy-start.1
  201.4 2.4 copy-start.1
  206.0 2.4 copy-start.1
  210.5 2.4 copy-start.1
  215.1 2.4 copy-start.1
  218.5 0.8 copy-start.2
  219.6 2.4 copy-start.1
  224.1 2.4 copy-start.1
  228.7 2.4 copy-start.1
  233.2 2.4 copy-start.1
  237.8 2.4 copy-start.1
  242.3 2.4 copy-start.1
  246.8 2.4 copy-start.1
  251.4 2.4 copy-start.1
  255.9 2.4 copy-start.1
  260.5 2.4 copy-start.1
  265.0 2.4 copy-start.1
  (15 other events, 12.0 us)
Sparse Core Ops, SparseCore 0:
  11.8 116.6 all-gather.2
  136.8 53.1 all-gather.4
where the time goes:
time: 298 us; the launch traced here: 297 us
  waiting for transfers between devices  163 us (55%)
  local copies, waits for them, and re-layouts  43.1 us (14%)
  matrix products  40.3 us (14%)
  blocking collectives  17.8 us (6%)
  other arithmetic  17.2 us (6%)
  between operations  14.3 us (5%)
    all_gather x1, waiting for transfers between devices, per_device(): piece = lax.all_gather(modulated, 'dp', axis=0, tiled=True)  117 us
    all_gather x1, waiting for transfers between devices, in_one_piece(): lax.all_gather(both, axis, axis=dim, tiled=True)  45.9 us
    dynamic_slice x16, local copies, waits for them, and re-layouts, single(): value_block = lax.dynamic_slice_in_dim(piece[1], index * tokc, tokc, 0)  18.1 us
    all_to_all x1, blocking collectives, per_device(): lax.all_to_all(result, 'dp', split_axis=0, concat_axis=1, tiled=True)  17.8 us
    dot_general x16, matrix products, update(): jnp.einsum('htk,khd->thd', weights.astype(jnp.bfloat16), value_block.resh...  17 us
    cond x80, local copies, waits for them, and re-layouts  12.7 us
    dot_general x16, matrix products, update(): jnp.einsum('thd,khd->htk', query, key_block.reshape(tokc, HEAD_DEV, HD),...  10.1 us
    reduce_sum x16, other arithmetic, update(): total = total * fade + jnp.sum(weights, axis=-1)  9.03 us
  transfers between devices with their start and end apart: 2, of which 2 were waited for; matrix products, arithmetic and copies ran while one was open for 2% of the time, Pallas kernels for 0%

commit v1 on v0

--- a/solution.py
+++ b/solution.py
@@ -1,3 +1,4 @@
+import functools
 import math
 import jax
 import jax.numpy as jnp
@@ -8,6 +9,17 @@
 HD = 128
 HEAD_DEV = 2
 STEPS = 16
+
+
+def _detail_screen(incoming_x, on_dim):
+    oldest = lax.axis_size("dp")
+    block_out = jnp.stack(oldest * [incoming_x], axis=0)
+    s_next = lax.all_to_all(block_out, concat_axis=0, axis_name="dp", split_axis=0)
+    view_out = jnp.concatenate(s_next, axis=on_dim)
+    return view_out
+
+
+produce_samples = functools.partial(_detail_screen, on_dim=0)
 
 
 def in_one_piece(arrays, axis, dim, along):
@@ -28,7 +40,7 @@
     picker = (steps[:, None] == jnp.arange(STEPS, dtype=jnp.int32)[None, :]).astype(jnp.float32)
     modulation = jnp.dot(picker, mod_table.reshape(STEPS, 2 * D), precision=lax.Precision.HIGHEST)
     modulated = (normed * (1.0 + modulation[:, :D]) + modulation[:, D:]).astype(jnp.bfloat16)
-    piece = lax.all_gather(modulated, "dp", axis=0, tiled=True)
+    piece = produce_samples(modulated)
     first = jnp.dot(piece, w_query, preferred_element_type=jnp.float32).astype(jnp.bfloat16)
     second = jnp.dot(piece, w_key, preferred_element_type=jnp.float32).astype(jnp.bfloat16)
     third = jnp.dot(piece, w_value, preferred_element_type=jnp.float32).astype(jnp.bfloat16)

time: 298 us -> 330 us (1.11)
  blocking collectives: 17.8 us -> 166 us
  waiting for transfers between devices: 163 us -> 46.5 us
    all_to_all x0 -> x1, blocking collectives: none -> 148 us  [_detail_screen(): lax.all_to_all(block_out, concat_axis=0, axis_name='dp', split_axis=0)]
    all_gather x1 -> x0, waiting for transfers between devices: 117 us -> none  [per_device(): piece = lax.all_gather(modulated, 'dp', axis=0, tiled=True)]
  transfers between devices with their start and end apart: 2 -> 1, of which waited for: 2 -> 1; matrix products, arithmetic and copies ran while one was open for 2% -> 2% of each run, Pallas kernels for 0% -> 0%
where the time goes in v1:
time: 330 us; the launch traced here: 329 us
  blocking collectives  166 us (50%)
  waiting for transfers between devices  46.5 us (14%)
  local copies, waits for them, and re-layouts  46.3 us (14%)
  matrix products  37.4 us (11%)
  other arithmetic  16.5 us (5%)
  between operations  14.3 us (4%)
    all_to_all x1, blocking collectives, _detail_screen(): lax.all_to_all(block_out, concat_axis=0, axis_name='dp', split_axis=0)  148 us
    all_gather x1, waiting for transfers between devices, in_one_piece(): lax.all_gather(both, axis, axis=dim, tiled=True)  46.5 us
    dynamic_slice x16, local copies, waits for them, and re-layouts, single(): value_block = lax.dynamic_slice_in_dim(piece[1], index * tokc, tokc, 0)  18.1 us
    all_to_all x1, blocking collectives, per_device(): lax.all_to_all(result, 'dp', split_axis=0, concat_axis=1, tiled=True)  17.6 us
    dot_general x16, matrix products, update(): jnp.einsum('htk,khd->thd', weights.astype(jnp.bfloat16), value_block.resh...  17 us
    cond x80, local copies, waits for them, and re-layouts  12.7 us
    dot_general x16, matrix products, update(): jnp.einsum('thd,khd->htk', query, key_block.reshape(tokc, HEAD_DEV, HD),...  10.1 us
    reduce_sum x16, other arithmetic, update(): total = total * fade + jnp.sum(weights, axis=-1)  9.03 us
  transfers between devices with their start and end apart: 1, of which 1 were waited for; matrix products, arithmetic and copies ran while one was open for 2% of the time, Pallas kernels for 0%

profile of v1, /device:TPU:27, one launch (start us, length us, event | category | flops | bytes accessed | tf_op | source)
XLA Modules:
  0.0 328.9 jit_solution(1734220689917225127)
XLA Ops:
  11.6 148.5 %all_to_all.18 = bf16[16,32,6144]{2,1,0:T(8,128)(2,1)S(1)} all-to-all(bf16[16,32,6144]{2,1,0:T(8,128)(2,1)S(1)} %stack.5), channel_id=1, replica_groups=mesh['group'=16,'dp'=16] {'dp'}, dimensions={0} | all-to-all | bytes 12582912 | tf_op jit(solution)/shard_map/all_to_all | solution.py:17
  160.1 1.9 convolution_convert_fusion.1
  164.3 1.8 convolution_convert_fusion.2
  167.0 6.3 %convolution_convert_fusion = bf16[512,256]{0,1:T(8,128)(2,1)} fusion(bf16[512,6144]{1,0:T(8,128)(2,1)} %bitcast.50, bf16[6144,256]{1,0:T(8,128)(2,1)} %param.15), kind=kOutput, calls=%fused_computation.21 | convolution fusion | flops 1610743808 | bytes 9699328 | tf_op jit(solution)/shard_map/dot_general | solution.py:44
  174.4 46.5 %all-gather.2.cloned.1.call-done = bf16[8192,512]{0,1:T(8,128)(2,1)} async-done(((bf16[512,512]{0,1:T(8,128)(2,1)}), bf16[8192,512]{0,1:T(8,128)(2,1)}) %all-gather.2.cloned.1.call-update) | async-done | bytes 8388624 | tf_op jit(solution)/shard_map/all_gather | solution.py:27
  220.9 5.9 %fusion.25 = (bf16[8192,256]{0,1:T(8,128)(2,1)}, bf16[8192,256]{0,1:T(8,128)(2,1)}) fusion(bf16[8192,512]{0,1:T(8,128)(2,1)} %all-gather.2.cloned.1.call-done), kind=kLoop, calls=%fused_computation.40 | loop fusion | bytes 16777216 | tf_op jit(solution)/shard_map/slice | solution.py:29
  227.6 72.5 %while.18 = (s32[]{:T(128)}, f32[2,512]{1,0:T(2,128)S(1)}, f32[2,512]{1,0:T(2,128)S(1)}, f32[512,2,128]{2,0,1:T(8,128)}, s32[]{:T(128)}, /*index=5*/bf16[8192,25...) while((s32[]{:T(128)}, f32[2,512]{1,0:T(2,128)S(1)}, ...), condition=%wide.region_6.7_spmd.clone, body=%wide.region_1.6_spmd.clone.sunk | while | flops 275778560 | bytes 14487929 | solution.py:99
  227.6 4.5 %conditional.3 = ((f32[2,512]{1,0:T(2,128)S(1)}, f32[2,512]{1,0:T(2,128)S(1)}, f32[512,2,128]{2,0,1:T(8,128)})) conditional(s32[]{:T(128)} %convert_element_type.70, (f32[2,512]{1,0:T(2,128)S(1)}, f32[2,512]{1,0:T(2,128)S(1)}, f32[512,2,128]{2,0,1:T(8,128)}) %tuple.61, (s32[512]{0:T(512)S(1)}, s32[]{:T(128)}, bf16[8192,256]{0,1:T(8,128)(2,1)}, ...), branch_computations={%region_2.0_spmd, %region_3.5_spmd} | conditional | flops 275778560 | bytes 14487690 | solution.py:82
  232.1 4.5 %conditional.3 = ((f32[2,512]{1,0:T(2,128)S(1)}, f32[2,512]{1,0:T(2,128)S(1)}, f32[512,2,128]{2,0,1:T(8,128)})) conditional(s32[]{:T(128)} %convert_element_type.70, (f32[2,512]{1,0:T(2,128)S(1)}, f32[2,512]{1,0:T(2,128)S(1)}, f32[512,2,128]{2,0,1:T(8,128)}) %tuple.61, (s32[512]{0:T(512)S(1)}, s32[]{:T(128)}, bf16[8192,256]{0,1:T(8,128)(2,1)}, ...), branch_computations={%region_2.0_spmd, %region_3.5_spmd} | conditional | flops 275778560 | bytes 14487690 | solution.py:82
  236.7 4.5 %conditional.3 = ((f32[2,512]{1,0:T(2,128)S(1)}, f32[2,512]{1,0:T(2,128)S(1)}, f32[512,2,128]{2,0,1:T(8,128)})) conditional(s32[]{:T(128)} %convert_element_type.70, (f32[2,512]{1,0:T(2,128)S(1)}, f32[2,512]{1,0:T(2,128)S(1)}, f32[512,2,128]{2,0,1:T(8,128)}) %tuple.61, (s32[512]{0:T(512)S(1)}, s32[]{:T(128)}, bf16[8192,256]{0,1:T(8,128)(2,1)}, ...), branch_computations={%region_2.0_spmd, %region_3.5_spmd} | conditional | flops 275778560 | bytes 14487690 | solution.py:82
  241.2 4.5 %conditional.3 = ((f32[2,512]{1,0:T(2,128)S(1)}, f32[2,512]{1,0:T(2,128)S(1)}, f32[512,2,128]{2,0,1:T(8,128)})) conditional(s32[]{:T(128)} %convert_element_type.70, (f32[2,512]{1,0:T(2,128)S(1)}, f32[2,512]{1,0:T(2,128)S(1)}, f32[512,2,128]{2,0,1:T(8,128)}) %tuple.61, (s32[512]{0:T(512)S(1)}, s32[]{:T(128)}, bf16[8192,256]{0,1:T(8,128)(2,1)}, ...), branch_computations={%region_2.0_spmd, %region_3.5_spmd} | conditional | flops 275778560 | bytes 14487690 | solution.py:82
  245.7 4.5 %conditional.3 = ((f32[2,512]{1,0:T(2,128)S(1)}, f32[2,512]{1,0:T(2,128)S(1)}, f32[512,2,128]{2,0,1:T(8,128)})) conditional(s32[]{:T(128)} %convert_element_type.70, (f32[2,512]{1,0:T(2,128)S(1)}, f32[2,512]{1,0:T(2,128)S(1)}, f32[512,2,128]{2,0,1:T(8,128)}) %tuple.61, (s32[512]{0:T(512)S(1)}, s32[]{:T(128)}, bf16[8192,256]{0,1:T(8,128)(2,1)}, ...), branch_computations={%region_2.0_spmd, %region_3.5_spmd} | conditional | flops 275778560 | bytes 14487690 | solution.py:82
  250.3 4.5 %conditional.3 = ((f32[2,512]{1,0:T(2,128)S(1)}, f32[2,512]{1,0:T(2,128)S(1)}, f32[512,2,128]{2,0,1:T(8,128)})) conditional(s32[]{:T(128)} %convert_element_type.70, (f32[2,512]{1,0:T(2,128)S(1)}, f32[2,512]{1,0:T(2,128)S(1)}, f32[512,2,128]{2,0,1:T(8,128)}) %tuple.61, (s32[512]{0:T(512)S(1)}, s32[]{:T(128)}, bf16[8192,256]{0,1:T(8,128)(2,1)}, ...), branch_computations={%region_2.0_spmd, %region_3.5_spmd} | conditional | flops 275778560 | bytes 14487690 | solution.py:82
  254.8 4.5 %conditional.3 = ((f32[2,512]{1,0:T(2,128)S(1)}, f32[2,512]{1,0:T(2,128)S(1)}, f32[512,2,128]{2,0,1:T(8,128)})) conditional(s32[]{:T(128)} %convert_element_type.70, (f32[2,512]{1,0:T(2,128)S(1)}, f32[2,512]{1,0:T(2,128)S(1)}, f32[512,2,128]{2,0,1:T(8,128)}) %tuple.61, (s32[512]{0:T(512)S(1)}, s32[]{:T(128)}, bf16[8192,256]{0,1:T(8,128)(2,1)}, ...), branch_computations={%region_2.0_spmd, %region_3.5_spmd} | conditional | flops 275778560 | bytes 14487690 | solution.py:82
  259.3 4.5 %conditional.3 = ((f32[2,512]{1,0:T(2,128)S(1)}, f32[2,512]{1,0:T(2,128)S(1)}, f32[512,2,128]{2,0,1:T(8,128)})) conditional(s32[]{:T(128)} %convert_element_type.70, (f32[2,512]{1,0:T(2,128)S(1)}, f32[2,512]{1,0:T(2,128)S(1)}, f32[512,2,128]{2,0,1:T(8,128)}) %tuple.61, (s32[512]{0:T(512)S(1)}, s32[]{:T(128)}, bf16[8192,256]{0,1:T(8,128)(2,1)}, ...), branch_computations={%region_2.0_spmd, %region_3.5_spmd} | conditional | flops 275778560 | bytes 14487690 | solution.py:82
  263.9 4.5 %conditional.3 = ((f32[2,512]{1,0:T(2,128)S(1)}, f32[2,512]{1,0:T(2,128)S(1)}, f32[512,2,128]{2,0,1:T(8,128)})) conditional(s32[]{:T(128)} %convert_element_type.70, (f32[2,512]{1,0:T(2,128)S(1)}, f32[2,512]{1,0:T(2,128)S(1)}, f32[512,2,128]{2,0,1:T(8,128)}) %tuple.61, (s32[512]{0:T(512)S(1)}, s32[]{:T(128)}, bf16[8192,256]{0,1:T(8,128)(2,1)}, ...), branch_computations={%region_2.0_spmd, %region_3.5_spmd} | conditional | flops 275778560 | bytes 14487690 | solution.py:82
  268.4 4.5 %conditional.3 = ((f32[2,512]{1,0:T(2,128)S(1)}, f32[2,512]{1,0:T(2,128)S(1)}, f32[512,2,128]{2,0,1:T(8,128)})) conditional(s32[]{:T(128)} %convert_element_type.70, (f32[2,512]{1,0:T(2,128)S(1)}, f32[2,512]{1,0:T(2,128)S(1)}, f32[512,2,128]{2,0,1:T(8,128)}) %tuple.61, (s32[512]{0:T(512)S(1)}, s32[]{:T(128)}, bf16[8192,256]{0,1:T(8,128)(2,1)}, ...), branch_computations={%region_2.0_spmd, %region_3.5_spmd} | conditional | flops 275778560 | bytes 14487690 | solution.py:82
  272.9 4.5 %conditional.3 = ((f32[2,512]{1,0:T(2,128)S(1)}, f32[2,512]{1,0:T(2,128)S(1)}, f32[512,2,128]{2,0,1:T(8,128)})) conditional(s32[]{:T(128)} %convert_element_type.70, (f32[2,512]{1,0:T(2,128)S(1)}, f32[2,512]{1,0:T(2,128)S(1)}, f32[512,2,128]{2,0,1:T(8,128)}) %tuple.61, (s32[512]{0:T(512)S(1)}, s32[]{:T(128)}, bf16[8192,256]{0,1:T(8,128)(2,1)}, ...), branch_computations={%region_2.0_spmd, %region_3.5_spmd} | conditional | flops 275778560 | bytes 14487690 | solution.py:82
  277.5 4.5 %conditional.3 = ((f32[2,512]{1,0:T(2,128)S(1)}, f32[2,512]{1,0:T(2,128)S(1)}, f32[512,2,128]{2,0,1:T(8,128)})) conditional(s32[]{:T(128)} %convert_element_type.70, (f32[2,512]{1,0:T(2,128)S(1)}, f32[2,512]{1,0:T(2,128)S(1)}, f32[512,2,128]{2,0,1:T(8,128)}) %tuple.61, (s32[512]{0:T(512)S(1)}, s32[]{:T(128)}, bf16[8192,256]{0,1:T(8,128)(2,1)}, ...), branch_computations={%region_2.0_spmd, %region_3.5_spmd} | conditional | flops 275778560 | bytes 14487690 | solution.py:82
  282.0 4.5 %conditional.3 = ((f32[2,512]{1,0:T(2,128)S(1)}, f32[2,512]{1,0:T(2,128)S(1)}, f32[512,2,128]{2,0,1:T(8,128)})) conditional(s32[]{:T(128)} %convert_element_type.70, (f32[2,512]{1,0:T(2,128)S(1)}, f32[2,512]{1,0:T(2,128)S(1)}, f32[512,2,128]{2,0,1:T(8,128)}) %tuple.61, (s32[512]{0:T(512)S(1)}, s32[]{:T(128)}, bf16[8192,256]{0,1:T(8,128)(2,1)}, ...), branch_computations={%region_2.0_spmd, %region_3.5_spmd} | conditional | flops 275778560 | bytes 14487690 | solution.py:82
  286.6 4.5 %conditional.3 = ((f32[2,512]{1,0:T(2,128)S(1)}, f32[2,512]{1,0:T(2,128)S(1)}, f32[512,2,128]{2,0,1:T(8,128)})) conditional(s32[]{:T(128)} %convert_element_type.70, (f32[2,512]{1,0:T(2,128)S(1)}, f32[2,512]{1,0:T(2,128)S(1)}, f32[512,2,128]{2,0,1:T(8,128)}) %tuple.61, (s32[512]{0:T(512)S(1)}, s32[]{:T(128)}, bf16[8192,256]{0,1:T(8,128)(2,1)}, ...), branch_computations={%region_2.0_spmd, %region_3.5_spmd} | conditional | flops 275778560 | bytes 14487690 | solution.py:82
  291.1 4.5 %conditional.3 = ((f32[2,512]{1,0:T(2,128)S(1)}, f32[2,512]{1,0:T(2,128)S(1)}, f32[512,2,128]{2,0,1:T(8,128)})) conditional(s32[]{:T(128)} %convert_element_type.70, (f32[2,512]{1,0:T(2,128)S(1)}, f32[2,512]{1,0:T(2,128)S(1)}, f32[512,2,128]{2,0,1:T(8,128)}) %tuple.61, (s32[512]{0:T(512)S(1)}, s32[]{:T(128)}, bf16[8192,256]{0,1:T(8,128)(2,1)}, ...), branch_computations={%region_2.0_spmd, %region_3.5_spmd} | conditional | flops 275778560 | bytes 14487690 | solution.py:82
  295.6 4.5 %conditional.3 = ((f32[2,512]{1,0:T(2,128)S(1)}, f32[2,512]{1,0:T(2,128)S(1)}, f32[512,2,128]{2,0,1:T(8,128)})) conditional(s32[]{:T(128)} %convert_element_type.70, (f32[2,512]{1,0:T(2,128)S(1)}, f32[2,512]{1,0:T(2,128)S(1)}, f32[512,2,128]{2,0,1:T(8,128)}) %tuple.61, (s32[512]{0:T(512)S(1)}, s32[]{:T(128)}, bf16[8192,256]{0,1:T(8,128)(2,1)}, ...), branch_computations={%region_2.0_spmd, %region_3.5_spmd} | conditional | flops 275778560 | bytes 14487690 | solution.py:82
  303.5 17.6 %all_to_all.19 = bf16[16,32,256]{2,1,0:T(8,128)(2,1)S(1)} all-to-all(bf16[16,32,256]{2,1,0:T(8,128)(2,1)S(1)} %convert_element_type.46), channel_id=1, replica_groups=mesh['group'=16,'dp'=16] {'dp'}, dimensions={0} | all-to-all | bytes 524288 | tf_op jit(solution)/shard_map/all_to_all | solution.py:102
  (221 shorter events, 84.4 us)
Async XLA Ops:
  6.5 153.6 %copy-start = (bf16[6144,256]{1,0:T(8,128)(2,1)S(1)}, bf16[6144,256]{1,0:T(8,128)(2,1)}, u32[]{:S(2)}) copy-start(bf16[6144,256]{1,0:T(8,128)(2,1)} %param.17) | copy-start | bytes 9437188
  6.5 214.4 %all-gather.2.cloned.1.call-start = ((), (), s32[]{:S(2)}) async-start(), calls=%async_computation.2 | async-start | bytes 8912896 | tf_op jit(solution)/shard_map/all_gather | solution.py:27
  6.5 4.1 %copy-start.4 = (bf16[1,32,6144]{2,1,0:T(8,128)(2,1)S(1)}, bf16[1,32,6144]{2,1,0:T(8,128)(2,1)}, u32[]{:S(2)}) copy-start(bf16[1,32,6144]{2,1,0:T(8,128)(2,1)} %param.11) | copy-start | bytes 1179652
  160.1 3.2 copy-start.1
  160.1 4.2 %copy-start.6 = (bf16[6144,256]{1,0:T(8,128)(2,1)S(1)}, bf16[6144,256]{1,0:T(8,128)(2,1)}, u32[]{:S(2)}) copy-start(bf16[6144,256]{1,0:T(8,128)(2,1)} %param.16) | copy-start | bytes 9437188
  174.4 53.2 %copy-start.5 = (s32[512]{0:T(512)S(1)}, s32[512]{0:T(512)}, u32[]{:S(2)}) copy-start(s32[512]{0:T(512)} %param.13) | copy-start | bytes 6148
  227.8 2.4 copy-start.2
  232.4 2.4 copy-start.2
  235.8 0.8 copy-start.3
  236.9 2.4 copy-start.2
  241.4 2.4 copy-start.2
  246.0 2.4 copy-start.2
  250.5 2.4 copy-start.2
  255.0 2.4 copy-start.2
  259.6 2.4 copy-start.2
  264.1 2.4 copy-start.2
  268.7 2.4 copy-start.2
  272.1 0.8 copy-start.3
  273.2 2.4 copy-start.2
  277.7 2.4 copy-start.2
  282.3 2.4 copy-start.2
  286.8 2.4 copy-start.2
  291.3 2.4 copy-start.2
  295.9 2.4 copy-start.2
  (14 other events, 11.1 us)
Sparse Core Ops, SparseCore 0:
  167.1 53.7 all-gather.1
